TPU v7x, 256 devices: a whole 4x4x8 slice. The times are simulated.
256 devices in a mesh: sub: 64 (over z, y, core), rhs: 4 (over x).
Axes of the slice: x: 4, y: 4, z: 8, core: 2. Of those that a mesh axis runs over, the one named last changes fastest.
Arguments:
- stiffness: float32 [3072, 4, 9216], P('sub'), may hold values from -1 to 2, as said below
- precond: float32 [3072, 9216], P('sub'), may hold values from -0.625 to 0.625
- rhs_vec: float32 [8, 294912], P('rhs', 'sub'), may hold values from -50 to 50
- cotangent: float32 [8, 294912], P('rhs', 'sub'), may hold values from -6 to 6
- col_index: int32 [3072, 4], P('sub'), may hold values from 0 to 59, as said below
- send_rows: int32 [64, 12], P('sub'), may hold values from 0 to 47, as said below
- counts: int32 [64], P('sub'), may hold values from 12 to 48, as said below
Outputs:
- solution: float32 [8, 294912], P('rhs', 'sub')
- grad_precond: float32 [3072, 9216], P('sub')
Inputs may be any that keep to these rules, and one draw needn't show every extreme that they name: `counts`: at least one subdomain has 48 live block rows. `send_rows`: for subdomain s, entries 0 to 5 are distinct live rows below counts[s] // 2 in increasing order, the first of them 0; entries 6 to 11 are distinct live rows from counts[s] // 2 on in increasing order, the last of them counts[s] - 1. Interface row j of the first group of subdomain s is coupled with interface row j of the second group of subdomain s - 1. `col_index`: index 6 + n is block n of the subdomain; indices below 6 and from 54 on are the blocks received from the previous and the next subdomain. Slot 0 of row n is 6 + n. A slot other than slot 0 that names 6 + n holds a zero block; rows that are not live hold only slot 0's block. `stiffness`: the operator A is symmetric and positive definite.
All inputs are finite; a program needn't handle non-finite values.
Results may differ from a plain program's by a relative error of at most 0.0003.
Values sent between devices are 32-bit elements; how exact they have to be, the bound alone decides.
A program may use at most 128 MiB of HBM per device.

v0:
```python
import jax
import jax.numpy as jnp
from jax import lax
from jax.sharding import PartitionSpec as P

BS = 96
K = 4
NBLK = 48
IF = 6
ITERS = 4
highest = lax.Precision.HIGHEST


def with_halo(array, sides, width):
    for axis, dim in sides:
        size, length = (lax.axis_size(axis), array.shape[dim])
        up = [(i, (i + 1) % size) for i in range(size - 1)]
        down = [(j, i) for i, j in up]
        last = lax.slice_in_dim(array, length - width, length, axis=dim)
        initial = lax.slice_in_dim(array, 0, width, axis=dim)
        before = lax.ppermute(last, axis, up)
        after = lax.ppermute(initial, axis, down)
        array = jnp.concatenate([before, array, after], axis=dim)
    return array


def local_dot(first_vec, second_vec):
    return jnp.sum(first_vec * second_vec, axis=(1, 2))


def widen(scalars):
    return scalars[:, None, None]


def precond_apply(weights, vector):
    projected = jnp.einsum("nab,rnb->rna", weights, vector, precision=highest)
    return (projected, vector + jnp.einsum("nab,rna->rnb", weights, projected, precision=highest))


def block_product(blocks, gathered):
    return jnp.einsum("nkab,rnkb->rna", blocks, gathered, precision=highest)


def stiff_apply(vector, blocks, columns, sending):
    outgoing = jnp.take(vector, sending, axis=1)
    framed = with_halo(outgoing, (("sub", 1),), IF)
    extended = jnp.concatenate([framed[:, :IF], vector, framed[:, 3 * IF :]], axis=1)
    return block_product(blocks, jnp.take(extended, columns, axis=1))


def norm_sum(first_vec, second_vec):
    return lax.psum(local_dot(first_vec, second_vec), "sub")


def grad_term(projected, zeta_bar, weight_zeta, resid_vec):
    first_part = jnp.einsum("rna,rnb->nab", projected, zeta_bar, precision=highest)
    return first_part + jnp.einsum("rna,rnb->nab", weight_zeta, resid_vec, precision=highest)


def shards(stiffness, precond, rhs_vec, cotangent, col_index, send_rows, counts):
    rhs_all, cot_all = (rhs_vec, cotangent)
    local_rhs = rhs_all.shape[0]
    blocks = stiffness.reshape(NBLK, K, BS, BS)
    weights = precond.reshape(NBLK, BS, BS)
    live_count = counts[0]
    sending = send_rows[0]
    live_mask = (jnp.arange(NBLK) < live_count).astype(jnp.float32)
    source = rhs_all.reshape(local_rhs, NBLK, BS) * live_mask[None, :, None]
    target = cot_all.reshape(local_rhs, NBLK, BS)
    residual = source
    first_proj, precon = precond_apply(weights, residual)
    first_res = residual
    direction = precon
    norm_now = norm_sum(residual, precon)
    solution = jnp.zeros_like(source)
    history = []
    for iteration in range(ITERS):
        applied = stiff_apply(direction, blocks, col_index, sending)
        curvature = lax.psum(local_dot(direction, applied), "sub")
        step_len = norm_now / curvature
        solution = solution + widen(step_len) * direction
        residual = residual - widen(step_len) * applied
        record = [direction, applied, step_len, curvature, norm_now]
        if iteration + 1 < ITERS:
            projected, precon = precond_apply(weights, residual)
            norm_next = norm_sum(residual, precon)
            ratio = norm_next / norm_now
            record = record + [residual, precon, projected, norm_next, ratio]
            direction = precon + widen(ratio) * direction
            norm_now = norm_next
        history.append(record)
    dir_bar = jnp.zeros_like(source)
    res_bar = jnp.zeros_like(source)
    norm_bar = jnp.zeros((local_rhs,), jnp.float32)
    grad_sum = jnp.zeros((NBLK, BS, BS), jnp.float32)
    for iteration in reversed(range(ITERS)):
        direction, applied, step_len, curvature, norm_now = history[iteration][:5]
        if iteration + 1 < ITERS:
            resid_next, precon, projected, norm_next, ratio = history[iteration][5:]
            ratio_bar, cot_dir = lax.psum(
                (local_dot(dir_bar, direction), local_dot(target, direction)), "sub"
            )
            norm_full = norm_bar + ratio_bar / norm_now
            zeta_bar = dir_bar + widen(norm_full) * resid_next
            weight_zeta, mapped = precond_apply(weights, zeta_bar)
            res_bar = res_bar + widen(norm_full) * precon + mapped
            res_image = lax.psum(local_dot(res_bar, applied), "sub")
            grad_sum = grad_sum + grad_term(projected, zeta_bar, weight_zeta, resid_next)
            dir_new = widen(ratio) * dir_bar
            norm_new = -ratio_bar * norm_next / (norm_now * norm_now)
        else:
            cot_dir = lax.psum(local_dot(target, direction), "sub")
            res_image = jnp.zeros_like(cot_dir)
            dir_new = jnp.zeros_like(source)
            norm_new = jnp.zeros_like(cot_dir)
        step_bar = cot_dir - res_image
        curv_bar = -step_bar * step_len / curvature
        dir_new = dir_new + widen(step_len) * target + widen(curv_bar) * applied
        image_bar = widen(curv_bar) * direction - widen(step_len) * res_bar
        dir_bar = dir_new + stiff_apply(image_bar, blocks, col_index, sending)
        norm_bar = norm_new + step_bar / curvature
    zeta_bar = dir_bar + widen(norm_bar) * first_res
    weight_zeta = jnp.einsum("nab,rnb->rna", weights, zeta_bar, precision=highest)
    grad_sum = grad_sum + grad_term(first_proj, zeta_bar, weight_zeta, first_res)
    grad_sum = lax.psum(grad_sum, "rhs")
    flat_solution = solution.reshape(local_rhs, NBLK * BS)
    return (flat_solution, grad_sum.reshape(NBLK, BS * BS))


def solution(mesh):
    in_specs = (
        P("sub", None, None),
        P("sub", None),
        P("rhs", "sub"),
        P("rhs", "sub"),
        P("sub", None),
        P("sub", None),
        P("sub"),
    )
    out_specs = (P("rhs", "sub"), P("sub", None))
    return jax.shard_map(shards, mesh=mesh, in_specs=in_specs, out_specs=out_specs, check_vma=False)
```

profile of v0, /device:TPU:1, one launch (start us, length us, event | category | flops | bytes accessed | tf_op | source)
XLA Modules:
  0.0 1994.4 jit_solution(11728397006781931206)
XLA Ops:
  12.3 3.8 convolution_bitcast_fusion.22
  18.9 4.6 collective-permute-start
  25.8 10.6 reshape.54
  37.3 10.5 multiply_reduce_fusion.16
  47.8 127.8 %all-reduce.4 = (f32[2]{0:T(128)S(1)}, f32[2]{0:T(128)S(1)}) all-reduce(f32[2]{0:T(128)S(1)} %get-tuple-element.10, f32[2]{0:T(128)S(1)} %get-tuple-element.9), channel_id=1, replica_groups=mesh['sub'=64,'rhs'=4] {'sub'}, use_global_device_ids=true, to_apply=%region_1.0 | all-reduce | flops 4 | bytes 32 | tf_op jit(solution)/shard_map/psum | solution.py:52
  175.8 3.8 convolution_bitcast_fusion.20
  181.7 127.4 %psum.135 = f32[2]{0:T(128)S(1)} all-reduce(f32[2]{0:T(128)S(1)} %get-tuple-element.44), channel_id=1, replica_groups=mesh['sub'=64,'rhs'=4] {'sub'}, use_global_device_ids=true, to_apply=%region_5.8 | all-reduce | flops 2 | bytes 16 | tf_op jit(solution)/shard_map/psum | solution.py:52
  314.3 2.5 collective-permute-done.3
  317.7 10.5 multiply_reduce_fusion.14
  328.2 122.2 %psum.136 = f32[2]{0:T(128)S(1)} all-reduce(f32[2]{0:T(128)S(1)} %get-tuple-element.46), channel_id=1, replica_groups=mesh['sub'=64,'rhs'=4] {'sub'}, use_global_device_ids=true, to_apply=%region_7.10 | all-reduce | flops 2 | bytes 16 | tf_op jit(solution)/shard_map/psum | solution.py:79
  450.5 3.8 convolution_bitcast_fusion.18
  456.5 125.9 %psum.137 = f32[2]{0:T(128)S(1)} all-reduce(f32[2]{0:T(128)S(1)} %get-tuple-element.48), channel_id=1, replica_groups=mesh['sub'=64,'rhs'=4] {'sub'}, use_global_device_ids=true, to_apply=%region_9.12 | all-reduce | flops 2 | bytes 16 | tf_op jit(solution)/shard_map/psum | solution.py:52
  587.5 2.5 collective-permute-done.5
  591.0 10.5 multiply_reduce_fusion.12
  601.5 122.2 %psum.138 = f32[2]{0:T(128)S(1)} all-reduce(f32[2]{0:T(128)S(1)} %get-tuple-element.50), channel_id=1, replica_groups=mesh['sub'=64,'rhs'=4] {'sub'}, use_global_device_ids=true, to_apply=%region_11.14 | all-reduce | flops 2 | bytes 16 | tf_op jit(solution)/shard_map/psum | solution.py:79
  723.8 3.8 convolution_bitcast_fusion.16
  729.8 125.9 %psum.139 = f32[2]{0:T(128)S(1)} all-reduce(f32[2]{0:T(128)S(1)} %get-tuple-element.52), channel_id=1, replica_groups=mesh['sub'=64,'rhs'=4] {'sub'}, use_global_device_ids=true, to_apply=%region_13.16 | all-reduce | flops 2 | bytes 16 | tf_op jit(solution)/shard_map/psum | solution.py:52
  864.3 11.1 multiply_reduce_fusion.1
  875.5 122.0 %all-reduce.3 = (f32[2]{0:T(128)S(1)}, f32[2]{0:T(128)S(1)}) all-reduce(f32[2]{0:T(128)S(1)} %get-tuple-element.6, f32[2]{0:T(128)S(1)} %get-tuple-element.5), channel_id=1, replica_groups=mesh['sub'=64,'rhs'=4] {'sub'}, use_global_device_ids=true, to_apply=%region_15.18 | all-reduce | flops 4 | bytes 32 | tf_op jit(solution)/shard_map/psum | solution.py:79
  1000.7 4.2 collective-permute-start.9
  1006.6 10.5 multiply_reduce_fusion.8
  1017.1 123.4 %psum.142 = f32[2]{0:T(128)S(1)} all-reduce(f32[2]{0:T(128)S(1)} %get-tuple-element.55), channel_id=1, replica_groups=mesh['sub'=64,'rhs'=4] {'sub'}, use_global_device_ids=true, to_apply=%region_19.22 | all-reduce | flops 2 | bytes 16 | tf_op jit(solution)/shard_map/psum | solution.py:100
  1140.6 3.8 convolution_bitcast_fusion.14
  1146.6 5.2 fusion.64
  1151.9 124.5 %all-reduce.2 = (f32[2]{0:T(128)S(1)}, f32[2]{0:T(128)S(1)}) all-reduce(f32[2]{0:T(128)S(1)} %copy-done.43, f32[2]{0:T(128)S(1)} %get-tuple-element.57), channel_id=1, replica_groups=mesh['sub'=64,'rhs'=4] {'sub'}, use_global_device_ids=true, to_apply=%region_21.24 | all-reduce | flops 4 | bytes 32 | tf_op jit(solution)/shard_map/psum | solution.py:100
  1279.7 2.6 collective-permute-start.11
  1282.2 5.4 fusion.63
  1288.6 10.5 multiply_reduce_fusion.5
  1299.1 123.0 %psum.145 = f32[2]{0:T(128)S(1)} all-reduce(f32[2]{0:T(128)S(1)} %get-tuple-element.59), channel_id=1, replica_groups=mesh['sub'=64,'rhs'=4] {'sub'}, use_global_device_ids=true, to_apply=%region_25.28 | all-reduce | flops 2 | bytes 16 | tf_op jit(solution)/shard_map/psum | solution.py:100
  1422.2 3.8 convolution_bitcast_fusion.12
  1428.2 5.2 fusion.66
  1433.5 125.2 %all-reduce.1 = (f32[2]{0:T(128)S(1)}, f32[2]{0:T(128)S(1)}) all-reduce(f32[2]{0:T(128)S(1)} %copy-done.42, f32[2]{0:T(128)S(1)} %get-tuple-element.61), channel_id=1, replica_groups=mesh['sub'=64,'rhs'=4] {'sub'}, use_global_device_ids=true, to_apply=%region_27.30 | all-reduce | flops 4 | bytes 32 | tf_op jit(solution)/shard_map/psum | solution.py:100
  1561.3 2.7 collective-permute-start.13
  1564.0 5.3 fusion.65
  1570.2 10.5 multiply_reduce_fusion.2
  1580.7 123.3 %psum.148 = f32[2]{0:T(128)S(1)} all-reduce(f32[2]{0:T(128)S(1)} %get-tuple-element.63), channel_id=1, replica_groups=mesh['sub'=64,'rhs'=4] {'sub'}, use_global_device_ids=true, to_apply=%region_31.34 | all-reduce | flops 2 | bytes 16 | tf_op jit(solution)/shard_map/psum | solution.py:100
  1704.1 3.8 convolution_bitcast_fusion.10
  1710.1 5.2 fusion.68
  1715.4 125.2 %all-reduce = (f32[2]{0:T(128)S(1)}, f32[2]{0:T(128)S(1)}) all-reduce(f32[2]{0:T(128)S(1)} %copy-done.41, f32[2]{0:T(128)S(1)} %get-tuple-element.65), channel_id=1, replica_groups=mesh['sub'=64,'rhs'=4] {'sub'}, use_global_device_ids=true, to_apply=%region_33.36 | all-reduce | flops 4 | bytes 32 | tf_op jit(solution)/shard_map/psum | solution.py:100
  1843.3 2.6 collective-permute-start.15
  1845.9 5.3 fusion.67
  1852.1 10.8 fusion.1
  1862.9 3.8 convolution_bitcast_fusion.8
  1866.7 3.9 fusion.69
  1870.6 4.3 add_add_fusion
  1874.9 2.5 reshape.57
  1878.2 106.4 %all-reduce.7.cloned.1.call-done = f32[48,9216]{1,0:T(8,128)} async-done(((f32[48,9216]{1,0:T(8,128)}), f32[48,9216]{1,0:T(8,128)}) %all-reduce.7.cloned.1.call-update) | async-done | bytes 1769488 | tf_op jit(solution)/shard_map/psum | solution.py:125
  1984.6 2.8 copy.72
  (208 shorter events, 61.8 us)
Async XLA Ops:
  7.2 1977.4 %all-reduce.7.cloned.1.call-start = ((), (), s32[]{:S(2)}) async-start(), calls=%async_computation | async-start | bytes 3538944 | tf_op jit(solution)/shard_map/psum | solution.py:125
  12.3 13.1 copy-start.13
  18.9 17.5 collective-permute-start
  23.5 12.9 collective-permute-start.1
  175.6 133.5 %copy-start.19 = (f32[2]{0:T(128)}, f32[2]{0:T(128)S(1)}, u32[]{:S(2)}) copy-start(f32[2]{0:T(128)S(1)} %get-tuple-element.19) | copy-start | bytes 28
  179.5 148.7 %copy-start.6 = (f32[2,48,96]{2,0,1:T(2,128)}, f32[2,48,96]{2,0,1:T(2,128)S(1)}, u32[]{:S(2)}) copy-start(f32[2,48,96]{2,0,1:T(2,128)S(1)} %convolution_bitcast_fusion.20) | copy-start | bytes 110596
  309.9 4.3 collective-permute-start.2
  311.8 4.9 collective-permute-start.3
  454.2 128.2 %copy-start.8 = (f32[2,48,96]{2,0,1:T(2,128)}, f32[2,48,96]{2,0,1:T(2,128)S(1)}, u32[]{:S(2)}) copy-start(f32[2,48,96]{2,0,1:T(2,128)S(1)} %convolution_bitcast_fusion.18) | copy-start | bytes 110596
  582.4 19.0 copy-start.16
  583.2 4.3 collective-permute-start.4
  585.1 4.9 collective-permute-start.5
  723.8 137.1 %copy-start.12 = (f32[2,4608]{1,0:T(2,128)S(1)}, f32[2,4608]{1,0:T(2,128)}, u32[]{:S(2)}) copy-start(f32[2,4608]{1,0:T(2,128)} %param.14) | copy-start | bytes 110596
  727.6 130.9 %copy-start.10 = (f32[2,48,96]{2,0,1:T(2,128)}, f32[2,48,96]{2,0,1:T(2,128)S(1)}, u32[]{:S(2)}) copy-start(f32[2,48,96]{2,0,1:T(2,128)S(1)} %convolution_bitcast_fusion.16) | copy-start | bytes 110596
  855.8 141.7 %copy-start.27 = (f32[2]{0:T(128)}, f32[2]{0:T(128)S(1)}, u32[]{:S(2)}) copy-start(f32[2]{0:T(128)S(1)} %psum.139) | copy-start | bytes 28
  855.8 19.7 copy-start.18
  856.5 4.5 collective-permute-start.6
  858.5 4.9 collective-permute-start.7
  998.8 6.2 collective-permute-start.8
  1000.7 4.9 collective-permute-start.9
  1006.6 134.0 %copy-start.38 = (f32[2]{0:T(128)S(1)}, f32[2]{0:T(128)}, u32[]{:S(2)}) copy-start(f32[2]{0:T(128)} %copy-done.37) | copy-start | bytes 28
  1006.6 133.9 %copy-start.40 = (f32[2]{0:T(128)S(1)}, f32[2]{0:T(128)}, u32[]{:S(2)}) copy-start(f32[2]{0:T(128)} %copy-done.39) | copy-start | bytes 28
  1144.4 132.0 %copy-start.25 = (f32[2]{0:T(128)S(1)}, f32[2]{0:T(128)}, u32[]{:S(2)}) copy-start(f32[2]{0:T(128)} %copy-done.24) | copy-start | bytes 28
  1144.4 137.8 %copy-start.11 = (f32[2,48,96]{2,0,1:T(2,128)S(1)}, f32[2,48,96]{2,0,1:T(2,128)}, u32[]{:S(2)}) copy-start(f32[2,48,96]{2,0,1:T(2,128)} %copy-done.10) | copy-start | bytes 110596
  1277.7 9.9 collective-permute-start.10
  1279.7 8.0 collective-permute-start.11
  1288.5 133.6 %copy-start.26 = (f32[2]{0:T(128)S(1)}, f32[2]{0:T(128)}, u32[]{:S(2)}) copy-start(f32[2]{0:T(128)} %copy-done.24) | copy-start | bytes 28
  1288.5 133.6 %copy-start.28 = (f32[2]{0:T(128)S(1)}, f32[2]{0:T(128)}, u32[]{:S(2)}) copy-start(f32[2]{0:T(128)} %copy-done.27) | copy-start | bytes 28
  1288.5 133.5 %copy-start.32 = (f32[2]{0:T(128)S(1)}, f32[2]{0:T(128)}, u32[]{:S(2)}) copy-start(f32[2]{0:T(128)} %copy-done.31) | copy-start | bytes 28
  1288.5 133.5 %copy-start.34 = (f32[2]{0:T(128)S(1)}, f32[2]{0:T(128)}, u32[]{:S(2)}) copy-start(f32[2]{0:T(128)} %copy-done.33) | copy-start | bytes 28
  1288.5 133.5 %copy-start.36 = (f32[2]{0:T(128)S(1)}, f32[2]{0:T(128)}, u32[]{:S(2)}) copy-start(f32[2]{0:T(128)} %copy-done.35) | copy-start | bytes 28
  1426.0 132.6 %copy-start.22 = (f32[2]{0:T(128)S(1)}, f32[2]{0:T(128)}, u32[]{:S(2)}) copy-start(f32[2]{0:T(128)} %copy-done.21) | copy-start | bytes 28
  1426.0 138.0 %copy-start.9 = (f32[2,48,96]{2,0,1:T(2,128)S(1)}, f32[2,48,96]{2,0,1:T(2,128)}, u32[]{:S(2)}) copy-start(f32[2,48,96]{2,0,1:T(2,128)} %copy-done.8) | copy-start | bytes 110596
  1428.2 142.0 %copy-start.17 = (f32[2]{0:T(128)S(1)}, f32[2]{0:T(128)}, u32[]{:S(2)}) copy-start(f32[2]{0:T(128)} %copy-done.16) | copy-start | bytes 28
  1559.4 9.9 collective-permute-start.12
  1561.3 8.0 collective-permute-start.13
  1570.2 133.8 %copy-start.20 = (f32[2]{0:T(128)S(1)}, f32[2]{0:T(128)}, u32[]{:S(2)}) copy-start(f32[2]{0:T(128)} %copy-done.19) | copy-start | bytes 28
  1570.2 133.8 %copy-start.23 = (f32[2]{0:T(128)S(1)}, f32[2]{0:T(128)}, u32[]{:S(2)}) copy-start(f32[2]{0:T(128)} %copy-done.21) | copy-start | bytes 28
  1570.2 133.8 %copy-start.30 = (f32[2]{0:T(128)S(1)}, f32[2]{0:T(128)}, u32[]{:S(2)}) copy-start(f32[2]{0:T(128)} %copy-done.29) | copy-start | bytes 28
  1707.9 132.6 %copy-start.45 = (f32[2]{0:T(128)S(1)}, f32[2]{0:T(128)}, u32[]{:S(2)}) copy-start(f32[2]{0:T(128)} %copy-done.44) | copy-start | bytes 28
  1707.9 138.0 %copy-start.7 = (f32[2,48,96]{2,0,1:T(2,128)S(1)}, f32[2,48,96]{2,0,1:T(2,128)}, u32[]{:S(2)}) copy-start(f32[2,48,96]{2,0,1:T(2,128)} %copy-done.6) | copy-start | bytes 110596
  1710.1 142.0 %copy-start.15 = (f32[2]{0:T(128)S(1)}, f32[2]{0:T(128)}, u32[]{:S(2)}) copy-start(f32[2]{0:T(128)} %copy-done.14) | copy-start | bytes 28
  1841.3 9.8 collective-permute-start.14
  1843.3 7.9 collective-permute-start.15
  1852.1 18.4 copy-start.2
  1852.1 18.4 copy-start.3
  1852.1 18.4 copy-start.4
  1852.1 18.4 copy-start.5
  (15 other events, 68.9 us)
Sparse Core Ops, SparseCore 0:
  1877.6 106.9 all-reduce.6
where the time goes:
time: 2000 us; the launch traced here: 1990 us
  blocking collectives  1620 us (81%)
  matrix products  170 us (8%)
  waiting for transfers between devices  115 us (6%)
  starting transfers between devices  39.2 us (2%)
  local copies, waits for them, and re-layouts  32.9 us (2%)
    psum x6, blocking collectives, shards(): lax.psum((local_dot(dir_bar, direction), local_dot(target, direction)), '...  745 us
    psum x4, blocking collectives, norm_sum(): return lax.psum(local_dot(first_vec, second_vec), 'sub')  507 us
    psum x3, blocking collectives, shards(): curvature = lax.psum(local_dot(direction, applied), 'sub')  366 us
    psum x1, waiting for transfers between devices, shards(): grad_sum = lax.psum(grad_sum, 'rhs')  106 us
    dot_general x8, matrix products, block_product(): return jnp.einsum('nkab,rnkb->rna', blocks, gathered, precision=highest)  84.9 us
  transfers between devices with their start and end apart: 17, of which 5 were waited for; matrix products, arithmetic and copies ran while one was open for 1% of the time, Pallas kernels for 0%

commit v1 on v0

--- a/solution.py
+++ b/solution.py
@@ -122,7 +122,9 @@
     zeta_bar = dir_bar + widen(norm_bar) * first_res
     weight_zeta = jnp.einsum("nab,rnb->rna", weights, zeta_bar, precision=highest)
     grad_sum = grad_sum + grad_term(first_proj, zeta_bar, weight_zeta, first_res)
-    grad_sum = lax.psum(grad_sum, "rhs")
+    grad_sum = grad_sum
+    for hop in (1, 2):
+        grad_sum = grad_sum + lax.ppermute(grad_sum, "rhs", [(dev, dev ^ hop) for dev in range(4)])
     flat_solution = solution.reshape(local_rhs, NBLK * BS)
     return (flat_solution, grad_sum.reshape(NBLK, BS * BS))
 

time: 2000 us -> 2030 us (1.015)
  the two profiles are of different devices: /device:TPU:1 before, /device:TPU:128 now
where the time goes in v1:
time: 2030 us; the launch traced here: 2020 us
  blocking collectives  1640 us (81%)
  matrix products  170 us (8%)
  waiting for transfers between devices  99.5 us (5%)
  starting transfers between devices  77.8 us (4%)
  local copies, waits for them, and re-layouts  31.1 us (2%)
    psum x6, blocking collectives, shards(): lax.psum((local_dot(dir_bar, direction), local_dot(target, direction)), '...  752 us
    psum x4, blocking collectives, norm_sum(): return lax.psum(local_dot(first_vec, second_vec), 'sub')  497 us
    psum x3, blocking collectives, shards(): curvature = lax.psum(local_dot(direction, applied), 'sub')  388 us
    ppermute x2, waiting for transfers between devices, shards(): lax.ppermute(grad_sum, 'rhs', [(dev, dev ^ hop) for dev in range(4)])  94.7 us
    dot_general x8, matrix products, block_product(): return jnp.einsum('nkab,rnkb->rna', blocks, gathered, precision=highest)  84.9 us
    ppermute x8, starting transfers between devices, with_halo(): after = lax.ppermute(initial, axis, down)  56.7 us
  transfers between devices with their start and end apart: 18, of which 6 were waited for; matrix products, arithmetic and copies ran while one was open for 1% of the time, Pallas kernels for 0%

profile of v1, /device:TPU:128, one launch (start us, length us, event | category | flops | bytes accessed | tf_op | source)
XLA Modules:
  0.0 2024.1 jit_solution(12514923845285997829)
XLA Ops:
  5.8 3.8 convolution_bitcast_fusion.22
  14.3 7.0 collective-permute-start.1
  21.6 10.6 reshape.54
  33.1 10.6 multiply_reduce_fusion.16
  43.6 124.5 %all-reduce.4 = (f32[2]{0:T(128)S(1)}, f32[2]{0:T(128)S(1)}) all-reduce(f32[2]{0:T(128)S(1)} %get-tuple-element.10, f32[2]{0:T(128)S(1)} %get-tuple-element.9), channel_id=1, replica_groups=mesh['sub'=64,'rhs'=4] {'sub'}, use_global_device_ids=true, to_apply=%region_1.0 | all-reduce | flops 4 | bytes 32 | tf_op jit(solution)/shard_map/psum | solution.py:52
  168.3 3.8 convolution_bitcast_fusion.20
  174.3 124.1 %psum.128 = f32[2]{0:T(128)S(1)} all-reduce(f32[2]{0:T(128)S(1)} %get-tuple-element.44), channel_id=1, replica_groups=mesh['sub'=64,'rhs'=4] {'sub'}, use_global_device_ids=true, to_apply=%region_5.8 | all-reduce | flops 2 | bytes 16 | tf_op jit(solution)/shard_map/psum | solution.py:52
  301.1 7.0 collective-permute-start.3
  310.3 10.5 multiply_reduce_fusion.14
  320.8 129.2 %psum.129 = f32[2]{0:T(128)S(1)} all-reduce(f32[2]{0:T(128)S(1)} %get-tuple-element.46), channel_id=1, replica_groups=mesh['sub'=64,'rhs'=4] {'sub'}, use_global_device_ids=true, to_apply=%region_7.10 | all-reduce | flops 2 | bytes 16 | tf_op jit(solution)/shard_map/psum | solution.py:79
  450.1 3.8 convolution_bitcast_fusion.18
  456.1 124.1 %psum.130 = f32[2]{0:T(128)S(1)} all-reduce(f32[2]{0:T(128)S(1)} %get-tuple-element.48), channel_id=1, replica_groups=mesh['sub'=64,'rhs'=4] {'sub'}, use_global_device_ids=true, to_apply=%region_9.12 | all-reduce | flops 2 | bytes 16 | tf_op jit(solution)/shard_map/psum | solution.py:52
  582.9 7.0 collective-permute-start.5
  592.1 10.5 multiply_reduce_fusion.12
  602.6 129.3 %psum.131 = f32[2]{0:T(128)S(1)} all-reduce(f32[2]{0:T(128)S(1)} %get-tuple-element.50), channel_id=1, replica_groups=mesh['sub'=64,'rhs'=4] {'sub'}, use_global_device_ids=true, to_apply=%region_11.14 | all-reduce | flops 2 | bytes 16 | tf_op jit(solution)/shard_map/psum | solution.py:79
  732.0 3.8 convolution_bitcast_fusion.16
  738.0 124.1 %psum.132 = f32[2]{0:T(128)S(1)} all-reduce(f32[2]{0:T(128)S(1)} %get-tuple-element.52), channel_id=1, replica_groups=mesh['sub'=64,'rhs'=4] {'sub'}, use_global_device_ids=true, to_apply=%region_13.16 | all-reduce | flops 2 | bytes 16 | tf_op jit(solution)/shard_map/psum | solution.py:52
  864.8 7.0 collective-permute-start.7
  874.0 11.1 multiply_reduce_fusion.1
  885.0 129.1 %all-reduce.3 = (f32[2]{0:T(128)S(1)}, f32[2]{0:T(128)S(1)}) all-reduce(f32[2]{0:T(128)S(1)} %get-tuple-element.6, f32[2]{0:T(128)S(1)} %get-tuple-element.5), channel_id=1, replica_groups=mesh['sub'=64,'rhs'=4] {'sub'}, use_global_device_ids=true, to_apply=%region_15.18 | all-reduce | flops 4 | bytes 32 | tf_op jit(solution)/shard_map/psum | solution.py:79
  1017.3 7.4 collective-permute-start.9
  1026.5 10.5 multiply_reduce_fusion.8
  1037.0 129.1 %psum.135 = f32[2]{0:T(128)S(1)} all-reduce(f32[2]{0:T(128)S(1)} %get-tuple-element.55), channel_id=1, replica_groups=mesh['sub'=64,'rhs'=4] {'sub'}, use_global_device_ids=true, to_apply=%region_19.22 | all-reduce | flops 2 | bytes 16 | tf_op jit(solution)/shard_map/psum | solution.py:100
  1166.2 3.8 convolution_bitcast_fusion.14
  1172.2 5.2 fusion.64
  1177.4 124.0 %all-reduce.2 = (f32[2]{0:T(128)S(1)}, f32[2]{0:T(128)S(1)}) all-reduce(f32[2]{0:T(128)S(1)} %copy-done.43, f32[2]{0:T(128)S(1)} %get-tuple-element.57), channel_id=1, replica_groups=mesh['sub'=64,'rhs'=4] {'sub'}, use_global_device_ids=true, to_apply=%region_21.24 | all-reduce | flops 4 | bytes 32 | tf_op jit(solution)/shard_map/psum | solution.py:100
  1304.7 7.1 collective-permute-start.11
  1311.9 5.4 fusion.63
  1318.2 10.5 multiply_reduce_fusion.5
  1328.7 125.1 %psum.138 = f32[2]{0:T(128)S(1)} all-reduce(f32[2]{0:T(128)S(1)} %get-tuple-element.59), channel_id=1, replica_groups=mesh['sub'=64,'rhs'=4] {'sub'}, use_global_device_ids=true, to_apply=%region_25.28 | all-reduce | flops 2 | bytes 16 | tf_op jit(solution)/shard_map/psum | solution.py:100
  1453.9 3.8 convolution_bitcast_fusion.12
  1459.9 5.2 fusion.66
  1465.2 124.0 %all-reduce.1 = (f32[2]{0:T(128)S(1)}, f32[2]{0:T(128)S(1)}) all-reduce(f32[2]{0:T(128)S(1)} %copy-done.42, f32[2]{0:T(128)S(1)} %get-tuple-element.61), channel_id=1, replica_groups=mesh['sub'=64,'rhs'=4] {'sub'}, use_global_device_ids=true, to_apply=%region_27.30 | all-reduce | flops 4 | bytes 32 | tf_op jit(solution)/shard_map/psum | solution.py:100
  1591.9 7.2 collective-permute-start.13
  1599.2 5.3 fusion.65
  1605.4 10.5 multiply_reduce_fusion.2
  1615.9 125.3 %psum.141 = f32[2]{0:T(128)S(1)} all-reduce(f32[2]{0:T(128)S(1)} %get-tuple-element.63), channel_id=1, replica_groups=mesh['sub'=64,'rhs'=4] {'sub'}, use_global_device_ids=true, to_apply=%region_31.34 | all-reduce | flops 2 | bytes 16 | tf_op jit(solution)/shard_map/psum | solution.py:100
  1741.3 3.8 convolution_bitcast_fusion.10
  1747.3 5.3 fusion.68
  1752.6 124.0 %all-reduce = (f32[2]{0:T(128)S(1)}, f32[2]{0:T(128)S(1)}) all-reduce(f32[2]{0:T(128)S(1)} %copy-done.41, f32[2]{0:T(128)S(1)} %get-tuple-element.65), channel_id=1, replica_groups=mesh['sub'=64,'rhs'=4] {'sub'}, use_global_device_ids=true, to_apply=%region_33.36 | all-reduce | flops 4 | bytes 32 | tf_op jit(solution)/shard_map/psum | solution.py:100
  1879.4 7.1 collective-permute-start.15
  1886.6 5.3 fusion.67
  1892.8 10.8 fusion.1
  1907.4 3.9 fusion.69
  1911.3 4.1 add_add_fusion
  1917.0 47.9 %collective-permute-done.16 = f32[48,96,96]{2,1,0:T(8,128)S(1)} collective-permute-done((f32[48,96,96]{2,1,0:T(8,128)S(1)}, f32[48,96,96]{2,1,0:T(8,128)S(1)}, u32[]{:S(2)}, u32[]{:S(2)}) %collective-permute-start.16) | collective-permute-done | bytes 1769504 | tf_op jit(solution)/shard_map/ppermute | solution.py:127
  1965.3 4.1 collective-permute-start.17
  1970.1 46.9 %collective-permute-done.17 = f32[48,96,96]{2,1,0:T(8,128)} collective-permute-done((f32[48,96,96]{2,1,0:T(8,128)S(1)}, f32[48,96,96]{2,1,0:T(8,128)}, u32[]{:S(2)}, u32[]{:S(2)}) %collective-permute-start.17) | collective-permute-done | bytes 1769504 | tf_op jit(solution)/shard_map/ppermute | solution.py:127
  (210 shorter events, 68.7 us)
Async XLA Ops:
  12.3 19.8 collective-permute-start
  14.3 17.9 collective-permute-start.1
  168.2 130.2 %copy-start.19 = (f32[2]{0:T(128)}, f32[2]{0:T(128)S(1)}, u32[]{:S(2)}) copy-start(f32[2]{0:T(128)S(1)} %get-tuple-element.19) | copy-start | bytes 28
  172.0 148.7 %copy-start.6 = (f32[2,48,96]{2,0,1:T(2,128)}, f32[2,48,96]{2,0,1:T(2,128)S(1)}, u32[]{:S(2)}) copy-start(f32[2,48,96]{2,0,1:T(2,128)S(1)} %convolution_bitcast_fusion.20) | copy-start | bytes 110596
  299.1 8.9 collective-permute-start.2
  301.1 8.3 collective-permute-start.3
  453.9 148.7 %copy-start.8 = (f32[2,48,96]{2,0,1:T(2,128)}, f32[2,48,96]{2,0,1:T(2,128)S(1)}, u32[]{:S(2)}) copy-start(f32[2,48,96]{2,0,1:T(2,128)S(1)} %convolution_bitcast_fusion.18) | copy-start | bytes 110596
  580.2 22.4 %copy-start.16 = (f32[2]{0:T(128)}, f32[2]{0:T(128)S(1)}, u32[]{:S(2)}) copy-start(f32[2]{0:T(128)S(1)} %div.66) | copy-start | bytes 28
  580.9 8.9 collective-permute-start.4
  582.9 8.3 collective-permute-start.5
  732.0 139.7 %copy-start.12 = (f32[2,4608]{1,0:T(2,128)S(1)}, f32[2,4608]{1,0:T(2,128)}, u32[]{:S(2)}) copy-start(f32[2,4608]{1,0:T(2,128)} %param.14) | copy-start | bytes 110596
  735.7 129.0 %copy-start.10 = (f32[2,48,96]{2,0,1:T(2,128)}, f32[2,48,96]{2,0,1:T(2,128)S(1)}, u32[]{:S(2)}) copy-start(f32[2,48,96]{2,0,1:T(2,128)S(1)} %convolution_bitcast_fusion.16) | copy-start | bytes 110596
  862.0 152.1 %copy-start.27 = (f32[2]{0:T(128)}, f32[2]{0:T(128)S(1)}, u32[]{:S(2)}) copy-start(f32[2]{0:T(128)S(1)} %psum.132) | copy-start | bytes 28
  862.0 23.0 %copy-start.18 = (f32[2]{0:T(128)}, f32[2]{0:T(128)S(1)}, u32[]{:S(2)}) copy-start(f32[2]{0:T(128)S(1)} %div.68) | copy-start | bytes 28
  862.8 9.0 collective-permute-start.6
  864.8 8.3 collective-permute-start.7
  1015.4 9.3 collective-permute-start.8
  1017.3 8.3 collective-permute-start.9
  1026.5 139.6 %copy-start.38 = (f32[2]{0:T(128)S(1)}, f32[2]{0:T(128)}, u32[]{:S(2)}) copy-start(f32[2]{0:T(128)} %copy-done.37) | copy-start | bytes 28
  1026.5 139.6 %copy-start.40 = (f32[2]{0:T(128)S(1)}, f32[2]{0:T(128)}, u32[]{:S(2)}) copy-start(f32[2]{0:T(128)} %copy-done.39) | copy-start | bytes 28
  1170.0 131.5 %copy-start.25 = (f32[2]{0:T(128)S(1)}, f32[2]{0:T(128)}, u32[]{:S(2)}) copy-start(f32[2]{0:T(128)} %copy-done.24) | copy-start | bytes 28
  1170.0 141.9 %copy-start.11 = (f32[2,48,96]{2,0,1:T(2,128)S(1)}, f32[2,48,96]{2,0,1:T(2,128)}, u32[]{:S(2)}) copy-start(f32[2,48,96]{2,0,1:T(2,128)} %copy-done.10) | copy-start | bytes 110596
  1302.8 14.4 collective-permute-start.10
  1304.7 12.5 collective-permute-start.11
  1318.2 135.6 %copy-start.26 = (f32[2]{0:T(128)S(1)}, f32[2]{0:T(128)}, u32[]{:S(2)}) copy-start(f32[2]{0:T(128)} %copy-done.24) | copy-start | bytes 28
  1318.2 135.6 %copy-start.28 = (f32[2]{0:T(128)S(1)}, f32[2]{0:T(128)}, u32[]{:S(2)}) copy-start(f32[2]{0:T(128)} %copy-done.27) | copy-start | bytes 28
  1318.2 135.6 %copy-start.32 = (f32[2]{0:T(128)S(1)}, f32[2]{0:T(128)}, u32[]{:S(2)}) copy-start(f32[2]{0:T(128)} %copy-done.31) | copy-start | bytes 28
  1318.2 135.6 %copy-start.34 = (f32[2]{0:T(128)S(1)}, f32[2]{0:T(128)}, u32[]{:S(2)}) copy-start(f32[2]{0:T(128)} %copy-done.33) | copy-start | bytes 28
  1318.2 135.6 %copy-start.36 = (f32[2]{0:T(128)S(1)}, f32[2]{0:T(128)}, u32[]{:S(2)}) copy-start(f32[2]{0:T(128)} %copy-done.35) | copy-start | bytes 28
  1457.7 131.5 %copy-start.22 = (f32[2]{0:T(128)S(1)}, f32[2]{0:T(128)}, u32[]{:S(2)}) copy-start(f32[2]{0:T(128)} %copy-done.21) | copy-start | bytes 28
  1457.7 141.5 %copy-start.9 = (f32[2,48,96]{2,0,1:T(2,128)S(1)}, f32[2,48,96]{2,0,1:T(2,128)}, u32[]{:S(2)}) copy-start(f32[2,48,96]{2,0,1:T(2,128)} %copy-done.8) | copy-start | bytes 110596
  1459.9 145.4 %copy-start.17 = (f32[2]{0:T(128)S(1)}, f32[2]{0:T(128)}, u32[]{:S(2)}) copy-start(f32[2]{0:T(128)} %copy-done.16) | copy-start | bytes 28
  1590.0 14.4 collective-permute-start.12
  1591.9 12.5 collective-permute-start.13
  1605.4 135.9 %copy-start.20 = (f32[2]{0:T(128)S(1)}, f32[2]{0:T(128)}, u32[]{:S(2)}) copy-start(f32[2]{0:T(128)} %copy-done.19) | copy-start | bytes 28
  1605.4 135.9 %copy-start.23 = (f32[2]{0:T(128)S(1)}, f32[2]{0:T(128)}, u32[]{:S(2)}) copy-start(f32[2]{0:T(128)} %copy-done.21) | copy-start | bytes 28
  1605.4 135.8 %copy-start.30 = (f32[2]{0:T(128)S(1)}, f32[2]{0:T(128)}, u32[]{:S(2)}) copy-start(f32[2]{0:T(128)} %copy-done.29) | copy-start | bytes 28
  1745.1 131.5 %copy-start.45 = (f32[2]{0:T(128)S(1)}, f32[2]{0:T(128)}, u32[]{:S(2)}) copy-start(f32[2]{0:T(128)} %copy-done.44) | copy-start | bytes 28
  1745.1 141.4 %copy-start.7 = (f32[2,48,96]{2,0,1:T(2,128)S(1)}, f32[2,48,96]{2,0,1:T(2,128)}, u32[]{:S(2)}) copy-start(f32[2,48,96]{2,0,1:T(2,128)} %copy-done.6) | copy-start | bytes 110596
  1747.3 145.4 %copy-start.15 = (f32[2]{0:T(128)S(1)}, f32[2]{0:T(128)}, u32[]{:S(2)}) copy-start(f32[2]{0:T(128)} %copy-done.14) | copy-start | bytes 28
  1877.5 14.4 collective-permute-start.14
  1879.4 12.4 collective-permute-start.15
  1892.8 18.4 copy-start.2
  1892.8 18.4 copy-start.3
  1892.8 18.4 copy-start.4
  1892.8 18.4 copy-start.5
  1915.4 49.4 %collective-permute-start.16 = (f32[48,96,96]{2,1,0:T(8,128)S(1)}, f32[48,96,96]{2,1,0:T(8,128)S(1)}, u32[]{:S(2)}, u32[]{:S(2)}) collective-permute-start(f32[48,96,96]{2,1,0:T(8,128)S(1)} %add_add_fusion), channel_id=1, source_target_pairs={{0,1},{1,0},{2,3},{3,2},{4,5},{5,4},{6,7},{7,6},{8,9},{9,8},{10,11... | collective-permute-start | bytes 5308424 | tf_op jit(solution)/shard_map/ppermute | solution.py:127
  1965.3 51.7 %collective-permute-start.17 = (f32[48,96,96]{2,1,0:T(8,128)S(1)}, f32[48,96,96]{2,1,0:T(8,128)}, u32[]{:S(2)}, u32[]{:S(2)}) collective-permute-start(f32[48,96,96]{2,1,0:T(8,128)S(1)} %add.235), channel_id=1, source_target_pairs={{0,2},{1,3},{2,0},{3,1},{4,6},{5,7},{6,4},{7,5},{8,10},{9,11},{10,... | collective-permute-start | bytes 5308424 | tf_op jit(solution)/shard_map/ppermute | solution.py:127
  (16 other events, 84.4 us)
